TPU v7x, 256 devices: a whole 4x4x8 slice. The times are simulated.
256 devices in a mesh: head: 16 (over z, core), tail: 16 (over y, x).
Axes of the slice: x: 4, y: 4, z: 8, core: 2. Of those that a mesh axis runs over, the one named last changes fastest.
Arguments:
- head_emb: bfloat16 [131072, 800], P(('head', 'tail')), may hold values from -48 to 48
- head_state: float32 [131072], P(('head', 'tail')), may hold values from 0.01 to 1
- tail_emb: bfloat16 [64, 128, 800], P('tail'), may hold values from -1.5 to 1.5
- tail_state: float32 [64, 128], P('tail'), may hold values from 0.01 to 1
- relation_emb: bfloat16 [1024, 800], replicated, may hold values from -3.5 to 3.5
- head_rows: int32 [1024, 256], P(('head', 'tail')), may hold values from 0 to 511
- relations: int32 [1024, 256], P(('head', 'tail')), may hold values from 0 to 1023
- tail_offsets: int32 [1024, 256], P(('head', 'tail')), may hold values from 0 to 127
- tail_owner: int32 [1024, 1], P(('head', 'tail')), may hold values from 0 to 15; in each aligned block of 4 rows (0 to 3, 4 to 7, ...) at most 2 rows name the same one
- tail_local: int32 [1024], P(('head', 'tail')), may hold values from 0 to 3
- block_count: int32 [256], P(('head', 'tail')), may hold values from 1 to 4, as said below
- neg_blocks: int32 [8], replicated, may hold values from 0 to 63, as said below
Outputs:
- head_new: bfloat16 [131072, 800], P(('head', 'tail'))
- head_state_new: float32 [131072], P(('head', 'tail'))
- tail_new: bfloat16 [64, 128, 800], P('tail')
- tail_state_new: float32 [64, 128], P('tail')
Inputs may be any that keep to these rules, and one draw needn't show every extreme that they name: `tail_owner`: no tail index owns the tail blocks of more than 2 edge block slots of one device, and in some devices one owns exactly 2. `block_count`: some device has all 4 slots live. `neg_blocks`: distinct tail blocks; the last tail block is always among them.
All inputs are finite; a program needn't handle non-finite values.
Results may differ from a plain program's by a relative error of at most 0.0012.
The roundings to bfloat16 on the way count: a program that leaves them out, or rounds other values in their place, can miss the bound.
Values may be sent and summed in bfloat16 or wider, within the bound.
A program may use at most 128 MiB of HBM per device.

v0:
```python
import math
import jax
import jax.numpy as jnp
from jax import lax
from jax.sharding import PartitionSpec as P

LEARN_RATE = 0.3


def complex_product(left, right):
    half_width = left.shape[-1] // 2
    left_re, left_im = (left[..., :half_width], left[..., half_width:])
    right_re, right_im = (right[..., :half_width], right[..., half_width:])
    return jnp.concatenate(
        [left_re * right_re - left_im * right_im, left_re * right_im + left_im * right_re], axis=-1
    )


def conj_product(left, right):
    half_width = left.shape[-1] // 2
    left_re, left_im = (left[..., :half_width], left[..., half_width:])
    right_re, right_im = (right[..., :half_width], right[..., half_width:])
    return jnp.concatenate(
        [left_re * right_re + left_im * right_im, left_im * right_re - left_re * right_im], axis=-1
    )


def row_adagrad(embedding, adagrad_state, gradient):
    state_next = adagrad_state + jnp.mean(gradient * gradient, axis=-1)
    updated = (
        embedding.astype(jnp.float32) - LEARN_RATE * gradient / jnp.sqrt(state_next)[..., None]
    )
    return (updated.astype(jnp.bfloat16), state_next)


def head_sum(tail_grad):
    return lax.psum(tail_grad, "head")


def per_device(
    head_emb,
    head_state,
    tail_emb,
    tail_state,
    relation_emb,
    head_rows,
    relations,
    tail_offsets,
    tail_owner,
    tail_local,
    block_count,
    neg_blocks,
):
    block_total = tail_local.shape[0]
    edge_count = head_rows.shape[1]
    row_width = head_emb.shape[1]
    span_rows = tail_emb.shape[1]
    owned_blocks = tail_emb.shape[0]
    peer_count = lax.axis_size("tail")
    tail_rank = lax.axis_index("tail")
    capacity = max(2, (2 * block_total + peer_count - 1) // peer_count)
    owner_rank = tail_owner[:, 0]
    positions = jnp.arange(block_total, dtype=jnp.int32)
    same_owner = owner_rank[:, None] == owner_rank[None, :]
    earlier = positions[None, :] < positions[:, None]
    slot_index = jnp.sum((same_owner & earlier).astype(jnp.int32), axis=1)
    slot_place = owner_rank * capacity + slot_index
    global_block = owner_rank * owned_blocks + tail_local
    partition = lax.all_gather(tail_emb, "tail", axis=0, tiled=True)
    chosen = jnp.take(partition, global_block, axis=0)
    mine_ids = neg_blocks - tail_rank * owned_blocks
    is_mine = (mine_ids >= 0) & (mine_ids < owned_blocks)
    own_negs = jnp.where(
        is_mine[:, None, None],
        jnp.take(tail_emb, jnp.clip(mine_ids, 0, owned_blocks - 1), axis=0),
        jnp.zeros((), jnp.bfloat16),
    )
    negatives = lax.psum(own_negs.astype(jnp.float32).astype(jnp.bfloat16), "tail").reshape(
        -1, row_width
    )
    total_edges = block_total * edge_count
    flat_rows = head_rows.reshape(-1)
    block_of = jnp.arange(total_edges, dtype=jnp.int32) // edge_count
    live_mask = (block_of < block_count[0]).astype(jnp.float32)
    tail_index = block_of * span_rows + tail_offsets.reshape(-1)
    tail_vectors = jnp.take(chosen.reshape(-1, row_width), tail_index, axis=0)
    relation_vectors = jnp.take(relation_emb, relations.reshape(-1), axis=0)
    head_vectors = jnp.take(head_emb, flat_rows, axis=0)
    query = complex_product(
        head_vectors.astype(jnp.float32), relation_vectors.astype(jnp.float32)
    ).astype(jnp.bfloat16)
    per_group = math.gcd(block_total, max(1, 512 // edge_count))
    group_rows = per_group * edge_count
    group_count = total_edges // group_rows

    def grouped(values):
        return values.reshape((group_count, group_rows) + values.shape[1:])

    def score_group(neg_total, group_items):
        query_rows, tail_rows, live_rows = group_items
        query_float = query_rows.astype(jnp.float32)
        positive = jnp.sum(query_float * tail_rows.astype(jnp.float32), axis=1)
        negative = lax.dot_general(
            query_rows, negatives, (((1,), (1,)), ((), ())), preferred_element_type=jnp.float32
        )
        largest = jnp.maximum(positive, jnp.max(negative, axis=1))
        pos_exp = jnp.exp(positive - largest)
        neg_exp = jnp.exp(negative - largest[:, None])
        denominator = pos_exp + jnp.sum(neg_exp, axis=1)
        pos_grad = (pos_exp / denominator - 1.0) * live_rows
        neg_grad = (neg_exp / denominator[:, None] * live_rows[:, None]).astype(jnp.bfloat16)
        query_grad = pos_grad[:, None] * tail_rows.astype(jnp.float32) + jnp.dot(
            neg_grad, negatives, preferred_element_type=jnp.float32
        )
        tail_part = pos_grad[:, None] * query_float
        neg_total = neg_total + lax.dot_general(
            neg_grad, query_rows, (((0,), (0,)), ((), ())), preferred_element_type=jnp.float32
        )
        return (neg_total, (query_grad, tail_part))

    neg_start = jnp.zeros((negatives.shape[0], row_width), jnp.float32)
    neg_part, (query_grad, tail_part) = lax.scan(
        score_group, neg_start, (grouped(query), grouped(tail_vectors), grouped(live_mask))
    )
    query_grad = query_grad.reshape(total_edges, row_width)
    tail_part = tail_part.reshape(total_edges, row_width)
    head_grad = (
        jnp.zeros(head_emb.shape, jnp.float32)
        .at[flat_rows]
        .add(conj_product(query_grad, relation_vectors.astype(jnp.float32)))
    )
    block_grad = (
        jnp.zeros((block_total * span_rows, row_width), jnp.float32)
        .at[tail_index]
        .add(tail_part)
        .astype(jnp.bfloat16)
    )
    outgoing = (
        jnp.zeros((peer_count * capacity, span_rows, row_width), jnp.bfloat16)
        .at[slot_place]
        .set(block_grad.reshape(block_total, span_rows, row_width))
    )
    outgoing = outgoing.reshape(peer_count, capacity, span_rows, row_width)
    slot_ids = (
        jnp.zeros((peer_count * capacity,), jnp.int32)
        .at[slot_place]
        .set(tail_local)
        .reshape(peer_count, capacity)
    )
    incoming, incoming_ids = (
        lax.all_to_all(outgoing, "tail", split_axis=0, concat_axis=0, tiled=True),
        lax.all_to_all(slot_ids, "tail", split_axis=0, concat_axis=0, tiled=True),
    )
    which_block = (
        incoming_ids.reshape(-1)[:, None] == jnp.arange(owned_blocks, dtype=jnp.int32)[None, :]
    ).astype(jnp.bfloat16)
    tail_grad = lax.dot_general(
        which_block,
        incoming.reshape(peer_count * capacity, span_rows * row_width),
        (((0,), (0,)), ((), ())),
        preferred_element_type=jnp.float32,
    )
    neg_weights = (
        (mine_ids[:, None] == jnp.arange(owned_blocks, dtype=jnp.int32)[None, :]) & is_mine[:, None]
    ).astype(jnp.float32)
    neg_all = lax.psum(neg_part, ("head", "tail"))
    tail_total = head_sum(tail_grad) + lax.dot_general(
        neg_weights,
        neg_all.reshape(neg_weights.shape[0], span_rows * row_width),
        (((0,), (0,)), ((), ())),
        precision=lax.Precision.HIGHEST,
        preferred_element_type=jnp.float32,
    )
    head_updated, head_state_updated = row_adagrad(head_emb, head_state, head_grad)
    tail_updated, tail_state_updated = row_adagrad(
        tail_emb, tail_state, tail_total.reshape(owned_blocks, span_rows, row_width)
    )
    return (head_updated, head_state_updated, tail_updated, tail_state_updated)


def solution(mesh):
    placed = (
        P(("head", "tail"), None),
        P(("head", "tail")),
        P("tail", None, None),
        P("tail", None),
        P(),
        P(("head", "tail"), None),
        P(("head", "tail"), None),
        P(("head", "tail"), None),
        P(("head", "tail"), None),
        P(("head", "tail")),
        P(("head", "tail")),
        P(),
    )
    return jax.shard_map(
        per_device,
        mesh=mesh,
        in_specs=placed,
        out_specs=(
            P(("head", "tail"), None),
            P(("head", "tail")),
            P("tail", None, None),
            P("tail", None),
        ),
        check_vma=False,
    )
```

profile of v0, /device:TPU:1, one launch (start us, length us, event | category | flops | bytes accessed | tf_op | source)
XLA Modules:
  0.0 729.9 jit_solution(752198037437776522)
XLA Ops:
  10.9 7.6 %all-to-all-start = ((s32[16,1,2]{2,1,0:T(1,128)}), s32[16,1,2]{2,1,0:T(1,128)S(1)}, u32[]{:S(2)}, u32[]{:S(2)}) async-start(s32[16,1,2]{2,1,0:T(1,128)} %bitcast.13), calls=%async_computation | async-start | bytes 16384 | tf_op jit(solution)/shard_map/all_to_all | solution.py:152
  21.5 3.8 copy.82
  26.1 3.1 copy.79
  29.3 5.3 gather_fusion.3
  34.5 5.3 gather_fusion
  48.7 62.8 %all-gather.2.cloned.1.call-done = bf16[64,128,800]{1,2,0:T(8,128)(2,1)} async-done(((bf16[4,128,800]{1,2,0:T(8,128)(2,1)}), bf16[64,128,800]{1,2,0:T(8,128)(2,1)}) %all-gather.2.cloned.1.call-update) | async-done | bytes 13107216 | tf_op jit(solution)/shard_map/all_gather | solution.py:69
  111.5 5.4 gather_fusion.2
  119.6 5.3 gather_fusion.4
  124.9 3.3 broadcast_select_fusion
  128.2 3.5 copy.84
  131.6 81.5 %all-reduce.4.cloned.1.call-done = bf16[1024,800]{1,0:T(8,128)(2,1)} async-done(((bf16[1024,800]{1,0:T(8,128)(2,1)}), bf16[1024,800]{1,0:T(8,128)(2,1)}) %all-reduce.4.cloned.1.call-update) | async-done | bytes 1638416 | tf_op jit(solution)/shard_map/psum | solution.py:78
  213.2 30.7 %while.17 = (s32[]{:T(128)}, f32[1024,800]{0,1:T(8,128)}, f32[2,512,800]{1,2,0:T(8,128)}, f32[2,512,800]{1,2,0:T(8,128)}, bf16[2,512,800]{1,2,0:T(8,128)(2,1)S(1...) while((s32[]{:T(128)}, f32[1024,800]{0,1:T(8,128)}, ...), condition=%wide.region_5.7_spmd.clone, body=%wide.region_1.6_spmd.clone.sunk | while | flops 2527675904 | bytes 74365712 | solution.py:122
  213.2 3.0 fusion.55
  223.6 4.5 select_add_fusion.2
  238.4 5.4 select_add_fusion.2
  243.9 4.4 copy.95
  248.2 10.8 %scatter_custom_fusion.2 = f32[512,800]{1,0:T(8,128)S(1)} fusion(s32[1024]{0:T(1024)S(1)} %bitcast.112, f32[1024,800]{1,0:T(8,128)} %bitcast.92, f32[]{:T(128)} %constant.133.clone.1), kind=kCustom, calls=%fused_computation.49 | custom fusion | flops 819200 | bytes 1638912 | tf_op jit(solution)/shard_map/scatter-add | solution.py:135
  261.7 3.6 broadcast_in_dim.108
  268.1 4.6 all-to-all-start.1
  272.8 4.9 copy.92
  277.7 6.1 reshape.276
  287.4 4.4 copy.85
  291.8 75.6 %all-to-all-done.1 = bf16[16,2,128,800]{2,3,1,0:T(8,128)(2,1)} async-done(((bf16[16,2,128,800]{2,3,1,0:T(8,128)(2,1)}), bf16[16,2,128,800]{2,3,1,0:T(8,128)(2,1)}, u32[]{:S(2)}, u32[]{:S(2)}) %all-to-all-start.1) | async-done | bytes 6553632 | tf_op jit(solution)/shard_map/all_to_all | solution.py:151
  367.4 11.0 %copy.91 = bf16[16,2,128,800]{3,2,1,0:T(8,128)(2,1)} copy(bf16[16,2,128,800]{2,3,1,0:T(8,128)(2,1)} %all-to-all-done.1) | data formatting | bytes 13107200 | tf_op jit(solution)/shard_map/all_to_all | solution.py:151
  378.5 13.6 %reshape.275 = bf16[32,102400]{1,0:T(8,128)(2,1)} reshape(bf16[16,2,128,800]{3,2,1,0:T(8,128)(2,1)} %copy.91) | data formatting | bytes 13107200 | tf_op jit(solution)/shard_map/reshape | solution.py:159
  392.1 5.1 fusion.20
  397.3 6.6 multiply_add_fusion
  403.9 10.9 %scatter_custom_fusion = f32[512,800]{1,0:T(8,128)S(1)} fusion(s32[1024]{0:T(1024)S(1)} %bitcast.113, f32[1024,400]{1,0:T(8,128)} %get-tuple-element.225, f32[]{:T(128)} %constant.164, f32[1024,400]{1,0:T(8,128)} %get-tuple-element.224, f32[]{:T(128)} %constant.133.clone.1), kind=kCustom, calls=%fused_computation.32 | custom fusion | flops 1638400 | bytes 4915208 | tf_op jit(solution)/shard_map/scatter-add | solution.py:130
  419.1 172.2 %all-reduce.8.cloned.1.call-done = f32[8,102400]{1,0:T(8,128)} async-done(((f32[8,102400]{1,0:T(8,128)}), f32[8,102400]{1,0:T(8,128)}) %all-reduce.8.cloned.1.call-update) | async-done | bytes 3276816 | tf_op jit(solution)/shard_map/psum | solution.py:166
  591.3 116.5 %all-reduce.6.cloned.1.call-done = f32[4,102400]{1,0:T(4,128)} async-done(((f32[4,102400]{1,0:T(4,128)}), f32[4,102400]{1,0:T(4,128)}) %all-reduce.6.cloned.1.call-update) | async-done | bytes 1638416 | tf_op jit(solution)/shard_map/psum | solution.py:37
  707.9 5.1 broadcast_multiply_fusion
  716.2 3.1 mul.157
  (125 shorter events, 56.6 us)
Async XLA Ops:
  7.2 12.1 %copy-start.3 = (bf16[4,128,800]{1,2,0:T(8,128)(2,1)S(1)}, bf16[4,128,800]{1,2,0:T(8,128)(2,1)}, u32[]{:S(2)}) copy-start(bf16[4,128,800]{1,2,0:T(8,128)(2,1)} %param.18) | copy-start | bytes 2457604
  7.2 104.3 %all-gather.2.cloned.1.call-start = ((), (), s32[]{:S(2)}) async-start(), calls=%async_computation.3 | async-start | bytes 13926400 | tf_op jit(solution)/shard_map/all_gather | solution.py:69
  10.9 257.2 %all-to-all-start = ((s32[16,1,2]{2,1,0:T(1,128)}), s32[16,1,2]{2,1,0:T(1,128)S(1)}, u32[]{:S(2)}, u32[]{:S(2)}) async-start(s32[16,1,2]{2,1,0:T(1,128)} %bitcast.13), calls=%async_computation | async-start | bytes 16384 | tf_op jit(solution)/shard_map/all_to_all | solution.py:152
  18.5 194.7 %all-reduce.4.cloned.1.call-start = ((), (), s32[]{:S(2)}) async-start(), calls=%async_computation.2 | async-start | bytes 3670016 | tf_op jit(solution)/shard_map/psum | solution.py:78
  21.5 3.8 copy-start.12
  21.5 3.9 copy-start.15
  21.5 3.9 copy-start.16
  21.5 3.9 copy-start.9
  26.1 3.1 copy-start.10
  42.4 1.8 copy-start.1
  44.2 3.1 copy-start.11
  45.4 1.9 copy-start.6
  213.2 3.1 copy-start.2
  213.2 3.9 copy-start.17
  216.2 4.1 copy-start
  216.2 2.7 copy-start.7
  220.3 1.8 copy-start.8
  228.1 3.1 copy-start.2
  228.1 3.9 copy-start.17
  231.1 4.1 copy-start
  231.1 2.7 copy-start.7
  235.2 1.8 copy-start.8
  268.1 99.3 %all-to-all-start.1 = ((bf16[16,2,128,800]{2,3,1,0:T(8,128)(2,1)}), bf16[16,2,128,800]{2,3,1,0:T(8,128)(2,1)}, u32[]{:S(2)}, u32[]{:S(2)}) async-start(bf16[16,2,128,800]{2,3,1,0:T(8,128)(2,1)} %bitcast.86), calls=%async_computation.1 | async-start | bytes 13107200 | tf_op jit(solution)/shard_map/all_to_all | solution.py:151
  272.7 318.6 %all-reduce.8.cloned.1.call-start = ((), (), s32[]{:S(2)}) async-start(), calls=%async_computation.5 | async-start | bytes 6553600 | tf_op jit(solution)/shard_map/psum | solution.py:166
  283.7 1.1 copy-start.4
  283.7 424.1 %all-reduce.6.cloned.1.call-start = ((), (), s32[]{:S(2)}) async-start(), calls=%async_computation.4 | async-start | bytes 3276800 | tf_op jit(solution)/shard_map/psum | solution.py:37
  403.9 11.1 %copy-start.13 = (f32[512]{0:T(512)S(1)}, f32[512]{0:T(512)}, u32[]{:S(2)}) copy-start(f32[512]{0:T(512)} %param.17) | copy-start | bytes 6148
  716.1 3.1 copy-start.14
  716.2 3.7 copy-start.5
Sparse Core Ops, SparseCore 0:
  10.4 101.0 all-gather.1
  114.9 98.2 all-reduce.3
  283.9 307.4 all-reduce.7
  593.6 114.2 all-reduce.5
where the time goes:
time: 731 us; the launch traced here: 730 us
  waiting for transfers between devices  509 us (70%)
  local copies, waits for them, and re-layouts  111 us (15%)
  other arithmetic  52.5 us (7%)
  matrix products  29.1 us (4%)
  between operations  14.8 us (2%)
  starting transfers between devices  12.4 us (2%)
    psum x1, waiting for transfers between devices, per_device(): neg_all = lax.psum(neg_part, ('head', 'tail'))  172 us
    psum x1, waiting for transfers between devices, head_sum(): return lax.psum(tail_grad, 'head')  117 us
    psum x1, waiting for transfers between devices, per_device(): lax.psum(own_negs.astype(jnp.float32).astype(jnp.bfloat16), 'tail')  81.5 us
    all_to_all x1, waiting for transfers between devices, per_device(): lax.all_to_all(outgoing, 'tail', split_axis=0, concat_axis=0, tiled=True)  75.6 us
    all_gather x1, waiting for transfers between devices, per_device(): partition = lax.all_gather(tail_emb, 'tail', axis=0, tiled=True)  62.8 us
  transfers between devices with their start and end apart: 6, of which 5 were waited for; matrix products, arithmetic and copies ran while one was open for 23% of the time, Pallas kernels for 0%

commit v1 on v0

--- a/solution.py
+++ b/solution.py
@@ -3,8 +3,13 @@
 import jax.numpy as jnp
 from jax import lax
 from jax.sharding import PartitionSpec as P
+from jax.lax import all_gather
 
 LEARN_RATE = 0.3
+
+
+def define_sheets_on_mesh(panel):
+    return jnp.sum(all_gather(panel, axis_name="head"), 0)
 
 
 def complex_product(left, right):
@@ -34,7 +39,7 @@
 
 
 def head_sum(tail_grad):
-    return lax.psum(tail_grad, "head")
+    return define_sheets_on_mesh(tail_grad)
 
 
 def per_device(

time: 731 us -> 837 us (1.15); the launches traced: 730 us -> 826 us
  waiting for transfers between devices: 509 us -> 599 us
  other arithmetic: 52.5 us -> 61.4 us
    psum x1 -> x0, waiting for transfers between devices: 117 us -> none  [head_sum(): return lax.psum(tail_grad, 'head')]
    all_gather x0 -> x1, waiting for transfers between devices: none -> 103 us  [define_sheets_on_mesh(): return jnp.sum(all_gather(panel, axis_name='head'), 0)]
    psum x1, waiting for transfers between devices: 172 us -> 260 us  [per_device(): neg_all = lax.psum(neg_part, ('head', 'tail'))]
    all_to_all x1, waiting for transfers between devices: 75.6 us -> 91.5 us  [per_device(): lax.all_to_all(outgoing, 'tail', split_axis=0, concat_axis=0, tiled=True)]
    reduce_sum x0 -> x1, other arithmetic: none -> 9.63 us  [define_sheets_on_mesh(): return jnp.sum(all_gather(panel, axis_name='head'), 0)]
  transfers between devices with their start and end apart: 6 -> 6, of which waited for: 5 -> 5; matrix products, arithmetic and copies ran while one was open for 23% -> 17% of each run, Pallas kernels for 0% -> 0%
where the time goes in v1:
time: 837 us; the launch traced here: 826 us
  waiting for transfers between devices  599 us (72%)
  local copies, waits for them, and re-layouts  116 us (14%)
  other arithmetic  61.4 us (7%)
  matrix products  22.6 us (3%)
  between operations  15 us (2%)
  starting transfers between devices  12.4 us (1%)
    psum x1, waiting for transfers between devices, per_device(): neg_all = lax.psum(neg_part, ('head', 'tail'))  260 us
    all_gather x1, waiting for transfers between devices, define_sheets_on_mesh(): return jnp.sum(all_gather(panel, axis_name='head'), 0)  103 us
    all_to_all x1, waiting for transfers between devices, per_device(): lax.all_to_all(outgoing, 'tail', split_axis=0, concat_axis=0, tiled=True)  91.5 us
    psum x1, waiting for transfers between devices, per_device(): lax.psum(own_negs.astype(jnp.float32).astype(jnp.bfloat16), 'tail')  81.5 us
    all_gather x1, waiting for transfers between devices, per_device(): partition = lax.all_gather(tail_emb, 'tail', axis=0, tiled=True)  62.8 us
  transfers between devices with their start and end apart: 6, of which 5 were waited for; matrix products, arithmetic and copies ran while one was open for 17% of the time, Pallas kernels for 0%

profile of v1, /device:TPU:1, one launch (start us, length us, event | category | flops | bytes accessed | tf_op | source)
XLA Modules:
  0.0 826.1 jit_solution(9198306023450606556)
XLA Ops:
  10.9 7.6 all-to-all-start
  21.5 3.8 copy.82
  26.1 3.1 copy.79
  29.3 5.3 gather_fusion.3
  34.5 5.3 gather_fusion
  48.8 62.8 %all-gather.5.cloned.1.call-done = bf16[64,128,800]{1,2,0:T(8,128)(2,1)} async-done(((bf16[4,128,800]{1,2,0:T(8,128)(2,1)}), bf16[64,128,800]{1,2,0:T(8,128)(2,1)}) %all-gather.5.cloned.1.call-update) | async-done | bytes 13107216 | tf_op jit(solution)/shard_map/all_gather | solution.py:74
  111.5 5.4 gather_fusion.2
  119.6 5.3 gather_fusion.4
  124.9 3.3 broadcast_select_fusion
  128.2 3.5 copy.84
  131.7 81.5 %all-reduce.3.cloned.1.call-done = bf16[1024,800]{1,0:T(8,128)(2,1)} async-done(((bf16[1024,800]{1,0:T(8,128)(2,1)}), bf16[1024,800]{1,0:T(8,128)(2,1)}) %all-reduce.3.cloned.1.call-update) | async-done | bytes 1638416 | tf_op jit(solution)/shard_map/psum | solution.py:83
  213.2 24.3 %while.17 = (s32[]{:T(128)}, f32[1024,800]{0,1:T(8,128)}, f32[2,512,800]{1,2,0:T(8,128)}, f32[2,512,800]{1,2,0:T(8,128)}, bf16[2,512,800]{1,2,0:T(8,128)(2,1)S(1...) while((s32[]{:T(128)}, f32[1024,800]{0,1:T(8,128)}, ...), condition=%wide.region_5.7_spmd.clone, body=%wide.region_1.6_spmd.clone.sunk | while | flops 2527675904 | bytes 118405488 | solution.py:127
  213.2 3.0 fusion.54
  225.3 3.0 fusion.54
  237.4 4.4 copy.95
  241.8 11.1 %scatter_custom_fusion.2 = f32[512,800]{1,0:T(8,128)S(1)} fusion(s32[1024]{0:T(1024)S(1)} %bitcast.114, f32[1024,800]{1,0:T(8,128)} %bitcast.94, f32[]{:T(128)} %constant.133.clone.1), kind=kCustom, calls=%fused_computation.50 | custom fusion | flops 819200 | bytes 1638912 | tf_op jit(solution)/shard_map/scatter-add | solution.py:140
  255.5 3.6 broadcast_in_dim.108
  261.8 4.6 all-to-all-start.1
  267.8 91.5 %all-to-all-done.1 = bf16[16,2,128,800]{2,3,1,0:T(8,128)(2,1)} async-done(((bf16[16,2,128,800]{2,3,1,0:T(8,128)(2,1)}), bf16[16,2,128,800]{2,3,1,0:T(8,128)(2,1)}, u32[]{:S(2)}, u32[]{:S(2)}) %all-to-all-start.1) | async-done | bytes 6553632 | tf_op jit(solution)/shard_map/all_to_all | solution.py:156
  359.3 11.0 %copy.91 = bf16[16,2,128,800]{3,2,1,0:T(8,128)(2,1)} copy(bf16[16,2,128,800]{2,3,1,0:T(8,128)(2,1)} %all-to-all-done.1) | data formatting | bytes 13107200 | tf_op jit(solution)/shard_map/all_to_all | solution.py:156
  370.3 13.6 %reshape.275 = bf16[32,102400]{1,0:T(8,128)(2,1)} reshape(bf16[16,2,128,800]{3,2,1,0:T(8,128)(2,1)} %copy.91) | data formatting | bytes 13107200 | tf_op jit(solution)/shard_map/reshape | solution.py:164
  383.9 5.1 convolution_bitcast_fusion
  389.1 5.0 copy.92
  394.2 6.0 reshape.276
  402.6 4.9 copy.85
  407.5 6.6 multiply_add_fusion
  414.1 10.9 %scatter_custom_fusion = f32[512,800]{1,0:T(8,128)S(1)} fusion(s32[1024]{0:T(1024)S(1)} %bitcast.115, f32[1024,400]{1,0:T(8,128)} %get-tuple-element.225, f32[]{:T(128)} %constant.164, f32[1024,400]{1,0:T(8,128)} %get-tuple-element.224, f32[]{:T(128)} %constant.133.clone.1), kind=kCustom, calls=%fused_computation.33 | custom fusion | flops 1638400 | bytes 4915208 | tf_op jit(solution)/shard_map/scatter-add | solution.py:135
  429.5 102.5 %all-gather.7.cloned.1.call-done = f32[16,4,102400]{2,1,0:T(4,128)} async-done(((f32[1,4,102400]{2,1,0:T(4,128)}), f32[16,4,102400]{2,1,0:T(4,128)}) %all-gather.7.cloned.1.call-update) | async-done | bytes 26214416 | tf_op jit(solution)/shard_map/all_gather | solution.py:12
  532.0 9.6 %reduce_sum.65 = f32[4,102400]{1,0:T(4,128)S(1)} reduce(f32[16,4,102400]{2,1,0:T(4,128)} %all-gather.7.cloned.1.call-done, f32[]{:T(128)} %constant.133.clone.1), dimensions={0}, to_apply=%region_12.14 | reduce | flops 6144000 | bytes 27852804 | tf_op jit(solution)/shard_map/reduce_sum | solution.py:12
  541.6 259.7 %all-reduce.5.cloned.1.call-done = f32[8,102400]{1,0:T(8,128)} async-done(((f32[8,102400]{1,0:T(8,128)}), f32[8,102400]{1,0:T(8,128)}) %all-reduce.5.cloned.1.call-update) | async-done | bytes 3276816 | tf_op jit(solution)/shard_map/psum | solution.py:171
  801.4 4.9 broadcast_multiply_fusion
  809.3 4.3 mul.159
  (138 shorter events, 58.7 us)
Async XLA Ops:
  7.2 12.1 %copy-start.2 = (bf16[4,128,800]{1,2,0:T(8,128)(2,1)S(1)}, bf16[4,128,800]{1,2,0:T(8,128)(2,1)}, u32[]{:S(2)}) copy-start(bf16[4,128,800]{1,2,0:T(8,128)(2,1)} %param.18) | copy-start | bytes 2457604
  7.2 104.3 %all-gather.5.cloned.1.call-start = ((), (), s32[]{:S(2)}) async-start(), calls=%async_computation.3 | async-start | bytes 13926400 | tf_op jit(solution)/shard_map/all_gather | solution.py:74
  10.9 250.9 %all-to-all-start = ((s32[16,1,2]{2,1,0:T(1,128)}), s32[16,1,2]{2,1,0:T(1,128)S(1)}, u32[]{:S(2)}, u32[]{:S(2)}) async-start(s32[16,1,2]{2,1,0:T(1,128)} %bitcast.13), calls=%async_computation | async-start | bytes 16384 | tf_op jit(solution)/shard_map/all_to_all | solution.py:157
  18.5 194.7 %all-reduce.3.cloned.1.call-start = ((), (), s32[]{:S(2)}) async-start(), calls=%async_computation.2 | async-start | bytes 3670016 | tf_op jit(solution)/shard_map/psum | solution.py:83
  21.5 3.9 copy-start.15
  21.5 3.9 copy-start.18
  21.5 3.9 copy-start.19
  21.5 3.9 copy-start.12
  26.1 3.1 copy-start.13
  42.4 1.9 copy-start
  44.2 3.1 copy-start.14
  45.4 1.9 copy-start.5
  213.2 3.0 copy-start.1
  216.2 1.9 copy-start.6
  218.1 1.9 copy-start.8
  218.1 2.5 copy-start.20
  220.0 2.0 copy-start.7
  220.6 2.8 copy-start.10
  222.0 1.7 copy-start.9
  225.3 3.0 copy-start.1
  228.3 1.9 copy-start.6
  230.2 1.9 copy-start.8
  230.2 2.5 copy-start.20
  232.1 2.0 copy-start.7
  232.7 2.8 copy-start.10
  234.1 1.7 copy-start.9
  261.8 97.5 %all-to-all-start.1 = ((bf16[16,2,128,800]{2,3,1,0:T(8,128)(2,1)}), bf16[16,2,128,800]{2,3,1,0:T(8,128)(2,1)}, u32[]{:S(2)}, u32[]{:S(2)}) async-start(bf16[16,2,128,800]{2,3,1,0:T(8,128)(2,1)} %bitcast.88), calls=%async_computation.1 | async-start | bytes 13107200 | tf_op jit(solution)/shard_map/all_to_all | solution.py:156
  266.5 265.5 %all-gather.7.cloned.1.call-start = ((), (), s32[]{:S(2)}) async-start(), calls=%async_computation.5 | async-start | bytes 27852800 | tf_op jit(solution)/shard_map/all_gather | solution.py:12
  389.1 412.3 %all-reduce.5.cloned.1.call-start = ((), (), s32[]{:S(2)}) async-start(), calls=%async_computation.4 | async-start | bytes 6553600 | tf_op jit(solution)/shard_map/psum | solution.py:171
  414.1 11.1 %copy-start.16 = (f32[512]{0:T(512)S(1)}, f32[512]{0:T(512)}, u32[]{:S(2)}) copy-start(f32[512]{0:T(512)} %param.17) | copy-start | bytes 6148
  809.3 6.0 copy-start.17
  809.3 6.6 copy-start.4
  (3 other events, 4.5 us)
Sparse Core Ops, SparseCore 0:
  10.4 101.0 all-gather.4
  114.9 98.2 all-reduce.2
  389.2 142.7 all-gather.6
  537.4 263.9 all-reduce.4
